TPU v7x, 32 devices: a whole 2x2x4 slice. The times are simulated.
32 devices in a mesh: groups: 2 (over x), col: 16 (over z, y, core).
Axes of the slice: x: 2, y: 2, z: 4, core: 2. Of those that a mesh axis runs over, the one named last changes fastest.
Arguments:
- features: bfloat16 [32, 8, 8192], P(('groups', 'col')), parts along dimension 0
- zone_ids: int32 [32], P(('groups', 'col')), parts along dimension 0, may hold values from 0 to 7, as said below
- golden_owner: int32 [16], P('groups'), parts along dimension 0, may hold values from 0 to 15, as said below
- defect_mask: int32 [32, 8, 128], P(('groups', 'col')), parts along dimension 0, may hold values 0 or 1
- kernels: bfloat16 [2, 576, 64], replicated, may hold values from -0.25 to 0.25
Outputs:
- score: float32 [32, 8, 128], P(('groups', 'col')), parts along dimension 0
There are 2 independent parts, one for each index of `groups`. A program takes and returns all parts, laid end to end along the dimension named above; an argument that names none is the same for every part. Nothing has to cross between parts.
Inputs may be any that keep to these rules, and one draw needn't show every extreme that they name: `zone_ids`: every zone holds at least one die. golden_owner[z] is a die of zone z.
All inputs are finite; a program needn't handle non-finite values. No bound on the sum of `defect_mask` on one device may be relied on, other than what follows from the above.
Results may differ from a plain program's by a relative error of at most 0.0039.
Values may be sent and summed in bfloat16 or wider, within the bound.
A program may use at most 64 MiB of HBM per device.

v0:
```python
import jax
import jax.numpy as jnp
from jax import lax
from jax.sharding import PartitionSpec as P

C = 64
SHIFT = 6
BOX = 5
Z = 8


def box_sum(plane):
    rows = plane.shape[0]
    cols = plane.shape[1]
    reach = BOX // 2
    padded = jnp.pad(plane, ((reach, reach), (reach, reach)))
    across = padded[0:rows]
    for offset in range(1, BOX):
        across = across + padded[offset : offset + rows]
    total = across[:, 0:cols]
    for offset in range(1, BOX):
        total = total + across[:, offset : offset + cols]
    return total


def channel_sum(values, chans):
    return jnp.sum(values.reshape(values.shape[0], -1, chans), axis=-1)


def align_golden(test_tile, golden_tile, chans):
    height, spread = test_tile.shape
    width = spread // chans
    side = 2 * SHIFT + 1
    test_f = test_tile.astype(jnp.float32)
    padded = jnp.pad(golden_tile, ((SHIFT, SHIFT), (SHIFT * chans, SHIFT * chans)))
    padded_f = padded.astype(jnp.float32)
    golden_sq = channel_sum(padded_f * padded_f, chans)
    self_energy = box_sum(channel_sum(test_f * test_f, chans))

    def row_step(carry, row_off):
        numer, denom = carry
        band = lax.dynamic_slice_in_dim(padded, row_off, height, 0).astype(jnp.float32)
        sq_band = lax.dynamic_slice_in_dim(golden_sq, row_off, height, 0)
        for col_off in range(side):
            moved = band[:, col_off * chans : col_off * chans + spread]
            cross = box_sum(channel_sum(test_f * moved, chans))
            other = box_sum(sq_band[:, col_off : col_off + width])
            expo = jnp.exp(32.0 * cross / jnp.sqrt(self_energy * other + 1e-05))
            numer = numer + jnp.repeat(expo, chans, axis=1) * moved
            denom = denom + expo
        return ((numer, denom), None)

    start = (jnp.zeros((height, spread), jnp.float32), jnp.zeros((height, width), jnp.float32))
    (numer, denom), _ = lax.scan(row_step, start, jnp.arange(side, dtype=jnp.int32))
    return numer / jnp.repeat(denom, chans, axis=1)


def conv_three(tile, kernel):
    height, width, chans = tile.shape
    padded = jnp.pad(tile, ((1, 1), (1, 1), (0, 0)))
    windows = []
    for tap in range(9):
        row_off = tap // 3
        col_off = tap % 3
        windows.append(
            padded[row_off : row_off + height, col_off : col_off + width].reshape(
                height * width, chans
            )
        )
    stacked = jnp.concatenate(windows, axis=1)
    total = jnp.dot(stacked, kernel, preferred_element_type=jnp.float32)
    return total.reshape(height, width, kernel.shape[1])


def body(features, zone_ids, golden_owner, defect_mask, kernels):
    height = features.shape[1]
    width = defect_mask.shape[2]
    my_zone = zone_ids[0]
    wanted = golden_owner[my_zone]
    piece = lax.all_gather(features, "col", axis=0, tiled=True)
    positions = jnp.arange(piece.shape[0], dtype=jnp.int32)
    chosen = jnp.where((positions == wanted)[:, None, None], piece, jnp.zeros_like(piece))
    golden = jnp.sum(chosen, axis=0, keepdims=True)
    test_tile = features[0]
    aligned = align_golden(test_tile, golden[0], C)
    residual = (
        (test_tile.astype(jnp.float32) - aligned).astype(jnp.bfloat16).reshape(height, width, C)
    )
    hidden = jax.nn.relu(conv_three(residual, kernels[0])).astype(jnp.bfloat16)
    refined = residual.astype(jnp.float32) + conv_three(hidden, kernels[1])
    energy = jnp.mean(refined * refined, axis=-1)
    masked = defect_mask[0].astype(jnp.float32)
    die_sum = jnp.sum(energy * masked)
    die_count = jnp.sum(masked)
    onehot = (jnp.arange(Z, dtype=jnp.int32) == my_zone).astype(jnp.float32)
    zone_sum, zone_count = lax.psum((onehot * die_sum, onehot * die_count), "col")
    zone_mean = zone_sum / jnp.maximum(zone_count, 1.0)
    mine = jnp.sum(onehot * zone_mean)
    return (energy / (mine + 0.01))[None]


def solution(mesh):
    in_specs = (
        P(("groups", "col"), None, None),
        P(("groups", "col")),
        P("groups"),
        P(("groups", "col"), None, None),
        P(),
    )
    out_specs = P(("groups", "col"), None, None)
    return jax.shard_map(body, mesh=mesh, in_specs=in_specs, out_specs=out_specs, check_vma=False)
```

profile of v0, /device:TPU:0, one launch (start us, length us, event | category | flops | bytes accessed | tf_op | source)
XLA Modules:
  0.0 422.0 jit_solution(12637861433031280978)
XLA Ops:
  11.4 42.3 %all-gather.2.cloned.1.call-done = bf16[16,8,8192]{2,1,0:T(8,128)(2,1)} async-done(((bf16[1,8,8192]{2,1,0:T(8,128)(2,1)}), bf16[16,8,8192]{2,1,0:T(8,128)(2,1)}) %all-gather.2.cloned.1.call-update) | async-done | bytes 2097168 | tf_op jit(solution)/shard_map/all_gather | solution.py:80
  53.7 2.0 select_reduce_fusion
  57.7 318.3 %while.15 = (s32[]{:T(128)}, f32[8,8192]{1,0:T(8,128)}, f32[8,128]{1,0:T(8,128)S(1)}, s32[13]{0:T(128)S(1)}, bf16[20,8960]{1,0:T(8,128)(2,1)}, /*index=5*/f32[8,...) while((s32[]{:T(128)}, f32[8,8192]{1,0:T(8,128)}, ...), condition=%wide.region_17.18_spmd.clone, body=%wide.region_3.17_spmd.clone.sunk | while | flops 3815698 | bytes 38420288 | solution.py:54
  61.1 1.3 slice_multiply_fusion.14
  79.7 2.4 fusion.283
  85.5 1.3 slice_multiply_fusion.14
  88.2 1.1 reshape.318
  104.1 2.5 fusion.283
  110.0 1.3 slice_multiply_fusion.14
  128.6 2.5 fusion.283
  134.5 1.3 slice_multiply_fusion.14
  153.1 2.5 fusion.283
  159.0 1.3 slice_multiply_fusion.14
  177.6 2.5 fusion.283
  183.4 1.3 slice_multiply_fusion.14
  202.1 2.5 fusion.283
  207.9 1.3 slice_multiply_fusion.14
  226.6 2.5 fusion.283
  232.4 1.3 slice_multiply_fusion.14
  251.1 2.5 fusion.283
  256.9 1.3 slice_multiply_fusion.14
  275.6 2.5 fusion.283
  281.4 1.3 slice_multiply_fusion.14
  300.1 2.5 fusion.283
  305.9 1.3 slice_multiply_fusion.14
  324.5 2.5 fusion.283
  330.4 1.3 slice_multiply_fusion.14
  349.0 2.5 fusion.283
  354.9 1.3 slice_multiply_fusion.14
  373.5 2.5 fusion.283
  380.5 1.3 fusion.234
  381.8 31.4 %all-reduce.30 = (f32[8]{0:T(128)S(1)}, f32[8]{0:T(128)S(1)}) all-reduce(f32[8]{0:T(128)S(1)} %get-tuple-element.221, f32[8]{0:T(128)S(1)} %get-tuple-element.220), channel_id=1, replica_groups=mesh['groups'=2,'col'=16] {'col'}, use_global_device_ids=true, to_apply=%region_20.21 | all-reduce | flops 16 | bytes 128 | tf_op jit(solution)/shard_map/psum | solution.py:96
  (1006 shorter events, 251.4 us)
Async XLA Ops:
  6.5 4.8 %copy-start.3 = (bf16[1,8,8192]{2,1,0:T(8,128)(2,1)S(1)}, bf16[1,8,8192]{2,1,0:T(8,128)(2,1)}, u32[]{:S(2)}) copy-start(bf16[1,8,8192]{2,1,0:T(8,128)(2,1)} %param.7) | copy-start | bytes 393220
  6.5 2.6 copy-start.7
  6.5 4.0 copy-start.6
  6.5 47.1 %all-gather.2.cloned.1.call-start = ((), (), s32[]{:S(2)}) async-start(), calls=%async_computation | async-start | bytes 2228224 | tf_op jit(solution)/shard_map/all_gather | solution.py:80
  57.7 4.7 %copy-start = (f32[8,8192]{1,0:T(8,128)}, f32[8,8192]{1,0:T(8,128)S(1)}, u32[]{:S(2)}) copy-start(f32[8,8192]{1,0:T(8,128)S(1)} %get-tuple-element.456) | copy-start | bytes 786436 | tf_op jit(solution)/shard_map/while
  79.7 2.4 copy-start.1
  82.1 4.7 %copy-start = (f32[8,8192]{1,0:T(8,128)}, f32[8,8192]{1,0:T(8,128)S(1)}, u32[]{:S(2)}) copy-start(f32[8,8192]{1,0:T(8,128)S(1)} %get-tuple-element.456) | copy-start | bytes 786436 | tf_op jit(solution)/shard_map/while
  104.1 2.5 copy-start.1
  106.6 4.7 %copy-start = (f32[8,8192]{1,0:T(8,128)}, f32[8,8192]{1,0:T(8,128)S(1)}, u32[]{:S(2)}) copy-start(f32[8,8192]{1,0:T(8,128)S(1)} %get-tuple-element.456) | copy-start | bytes 786436 | tf_op jit(solution)/shard_map/while
  128.6 2.5 copy-start.1
  131.1 4.7 %copy-start = (f32[8,8192]{1,0:T(8,128)}, f32[8,8192]{1,0:T(8,128)S(1)}, u32[]{:S(2)}) copy-start(f32[8,8192]{1,0:T(8,128)S(1)} %get-tuple-element.456) | copy-start | bytes 786436 | tf_op jit(solution)/shard_map/while
  153.1 2.5 copy-start.1
  155.6 4.7 %copy-start = (f32[8,8192]{1,0:T(8,128)}, f32[8,8192]{1,0:T(8,128)S(1)}, u32[]{:S(2)}) copy-start(f32[8,8192]{1,0:T(8,128)S(1)} %get-tuple-element.456) | copy-start | bytes 786436 | tf_op jit(solution)/shard_map/while
  177.6 2.5 copy-start.1
  180.1 4.7 %copy-start = (f32[8,8192]{1,0:T(8,128)}, f32[8,8192]{1,0:T(8,128)S(1)}, u32[]{:S(2)}) copy-start(f32[8,8192]{1,0:T(8,128)S(1)} %get-tuple-element.456) | copy-start | bytes 786436 | tf_op jit(solution)/shard_map/while
  202.1 2.5 copy-start.1
  204.6 4.7 %copy-start = (f32[8,8192]{1,0:T(8,128)}, f32[8,8192]{1,0:T(8,128)S(1)}, u32[]{:S(2)}) copy-start(f32[8,8192]{1,0:T(8,128)S(1)} %get-tuple-element.456) | copy-start | bytes 786436 | tf_op jit(solution)/shard_map/while
  226.6 2.5 copy-start.1
  229.1 4.7 %copy-start = (f32[8,8192]{1,0:T(8,128)}, f32[8,8192]{1,0:T(8,128)S(1)}, u32[]{:S(2)}) copy-start(f32[8,8192]{1,0:T(8,128)S(1)} %get-tuple-element.456) | copy-start | bytes 786436 | tf_op jit(solution)/shard_map/while
  251.1 2.5 copy-start.1
  253.6 4.7 %copy-start = (f32[8,8192]{1,0:T(8,128)}, f32[8,8192]{1,0:T(8,128)S(1)}, u32[]{:S(2)}) copy-start(f32[8,8192]{1,0:T(8,128)S(1)} %get-tuple-element.456) | copy-start | bytes 786436 | tf_op jit(solution)/shard_map/while
  275.6 2.5 copy-start.1
  278.1 4.7 %copy-start = (f32[8,8192]{1,0:T(8,128)}, f32[8,8192]{1,0:T(8,128)S(1)}, u32[]{:S(2)}) copy-start(f32[8,8192]{1,0:T(8,128)S(1)} %get-tuple-element.456) | copy-start | bytes 786436 | tf_op jit(solution)/shard_map/while
  300.1 2.5 copy-start.1
  302.6 4.7 %copy-start = (f32[8,8192]{1,0:T(8,128)}, f32[8,8192]{1,0:T(8,128)S(1)}, u32[]{:S(2)}) copy-start(f32[8,8192]{1,0:T(8,128)S(1)} %get-tuple-element.456) | copy-start | bytes 786436 | tf_op jit(solution)/shard_map/while
  324.5 2.5 copy-start.1
  327.1 4.7 %copy-start = (f32[8,8192]{1,0:T(8,128)}, f32[8,8192]{1,0:T(8,128)S(1)}, u32[]{:S(2)}) copy-start(f32[8,8192]{1,0:T(8,128)S(1)} %get-tuple-element.456) | copy-start | bytes 786436 | tf_op jit(solution)/shard_map/while
  349.0 2.5 copy-start.1
  351.6 4.7 %copy-start = (f32[8,8192]{1,0:T(8,128)}, f32[8,8192]{1,0:T(8,128)S(1)}, u32[]{:S(2)}) copy-start(f32[8,8192]{1,0:T(8,128)S(1)} %get-tuple-element.456) | copy-start | bytes 786436 | tf_op jit(solution)/shard_map/while
  373.5 2.5 copy-start.1
  376.0 1.0 copy-start.2
  376.0 1.0 copy-start.4
  (1 other events, 0.9 us)
Sparse Core Ops, SparseCore 0:
  9.5 44.0 all-gather.1
where the time goes:
time: 425 us; the launch traced here: 422 us
  local copies, waits for them, and re-layouts  179 us (42%)
  other arithmetic  125 us (29%)
  waiting for transfers between devices  43 us (10%)
  blocking collectives  31.4 us (7%)
  loops' own time  27.6 us (6%)
  between operations  15 us (4%)
    reshape x170, local copies, waits for them, and re-layouts, channel_sum(): return jnp.sum(values.reshape(values.shape[0], -1, chans), axis=-1)  73.2 us
    reshape x169, local copies, waits for them, and re-layouts, row_step(): numer = numer + jnp.repeat(expo, chans, axis=1) * moved  59 us
    all_gather x1, waiting for transfers between devices, body(): piece = lax.all_gather(features, 'col', axis=0, tiled=True)  42.3 us
    reduce_sum x171, other arithmetic, channel_sum(): return jnp.sum(values.reshape(values.shape[0], -1, chans), axis=-1)  35.9 us
    add x13, other arithmetic, row_step(): numer = numer + jnp.repeat(expo, chans, axis=1) * moved  32.5 us
    broadcast_in_dim x169, local copies, waits for them, and re-layouts, row_step(): numer = numer + jnp.repeat(expo, chans, axis=1) * moved  32.3 us
    psum x1, blocking collectives, body(): lax.psum((onehot * die_sum, onehot * die_count), 'col')  31.4 us
    another operation x1, loops' own time, align_golden(): lax.scan(row_step, start, jnp.arange(side, dtype=jnp.int32))  27.6 us
  transfers between devices with their start and end apart: 1, of which 1 were waited for; matrix products, arithmetic and copies ran while one was open for 1% of the time, Pallas kernels for 0%

commit v1 on v0

v1 whole, which is shorter than its diff:
```python
import functools

import jax
import jax.numpy as jnp
from jax import lax
from jax.experimental import pallas as pl
from jax.experimental.pallas import tpu as pltpu
from jax.sharding import PartitionSpec as P

C = 64
H = 8
W = 128
SHIFT = 6
REACH = 2
Z = 8
MESH = pl.DeviceIdType.MESH


def gather_kernel(n, nz, ny, zone_ref, owner_ref, t_ref, g_ref, slots, own_sem, recv, sends):
    me = lax.axis_index("col")
    core = lax.rem(me, 2)
    yy = lax.rem(me // 2, ny)
    zz = me // (2 * ny)

    def idx(z, y, c):
        return (z * ny + y) * 2 + c

    up = idx(zz + 1, yy, core)
    down = idx(zz - 1, yy, core)
    side = idx(zz, 1 - yy, core)
    mate = idx(zz, yy, 1 - core)
    has_up = zz + 1 < nz
    has_down = zz > 0

    barrier = pltpu.get_barrier_semaphore()

    def greet(dev):
        pl.semaphore_signal(barrier, inc=1, device_id={"col": dev}, device_id_type=MESH)

    @pl.when(has_up)
    def _():
        greet(up)

    @pl.when(has_down)
    def _():
        greet(down)

    if ny == 2:
        greet(side)
    greet(mate)
    peers = ny + jnp.where(has_up, 1, 0) + jnp.where(has_down, 1, 0)
    pl.semaphore_wait(barrier, peers)

    def copy(kind, slot, dev, src=None):
        return pltpu.make_async_remote_copy(
            src_ref=slots.at[slot] if src is None else src,
            dst_ref=slots.at[slot],
            send_sem=sends.at[kind, slot],
            recv_sem=recv.at[slot],
            device_id={"col": dev},
            device_id_type=MESH,
        )

    def arrive(slot):
        copy(0, slot, mate).wait_recv()

    @pl.when(has_up)
    def _():
        copy(0, me, up, t_ref).start()

    @pl.when(has_down)
    def _():
        copy(1, me, down, t_ref).start()

    if ny == 2:
        copy(2, me, side, t_ref).start()
    copy(3, me, mate, t_ref).start()
    own = pltpu.make_async_copy(t_ref, slots.at[me], own_sem)
    own.start()

    def from_side(z):
        slot = idx(z, 1 - yy, core)
        arrive(slot)
        copy(3, slot, mate).start()

    for s in range(1, nz):
        below = zz - s
        above = zz + s

        @pl.when(below >= 0)
        def _():
            slot = idx(below, yy, core)
            arrive(slot)

            @pl.when(has_up)
            def _():
                copy(0, slot, up).start()

            if ny == 2:
                copy(2, slot, side).start()
            copy(3, slot, mate).start()

        @pl.when(above < nz)
        def _():
            slot = idx(above, yy, core)
            arrive(slot)

            @pl.when(has_down)
            def _():
                copy(1, slot, down).start()

            if ny == 2:
                copy(2, slot, side).start()
            copy(3, slot, mate).start()

        if ny == 2:
            if s == 1:
                from_side(zz)
            else:

                @pl.when(zz - (s - 1) >= 0)
                def _():
                    from_side(zz - (s - 1))

                @pl.when(zz + (s - 1) < nz)
                def _():
                    from_side(zz + (s - 1))

    if ny == 2:

        @pl.when(zz - (nz - 1) >= 0)
        def _():
            from_side(zz - (nz - 1))

        @pl.when(zz + (nz - 1) < nz)
        def _():
            from_side(zz + (nz - 1))

    for z in range(nz):
        for y in range(ny):
            arrive(idx(z, y, 1 - core))
    own.wait()

    def sent(kind, slot):
        copy(kind, slot, mate).wait_send()

    for z in range(nz):
        slot = idx(z, yy, core)

        @pl.when(jnp.logical_and(has_up, z <= zz))
        def _():
            sent(0, slot)

        @pl.when(jnp.logical_and(has_down, z >= zz))
        def _():
            sent(1, slot)

        if ny == 2:
            sent(2, slot)
        for y in range(ny):
            sent(3, idx(z, y, core))

    g_ref[...] = slots[owner_ref[zone_ref[0]]]


def gather_golden(zone, owners, tile, n):
    ny = 2 if n == 16 else 1
    nz = n // (2 * ny)
    return pl.pallas_call(
        functools.partial(gather_kernel, n, nz, ny),
        out_shape=jax.ShapeDtypeStruct(tile.shape, tile.dtype),
        in_specs=[
            pl.BlockSpec(memory_space=pltpu.SMEM),
            pl.BlockSpec(memory_space=pltpu.SMEM),
            pl.BlockSpec(memory_space=pltpu.VMEM),
        ],
        out_specs=pl.BlockSpec(memory_space=pltpu.VMEM),
        scratch_shapes=[
            pltpu.VMEM((n,) + tile.shape, tile.dtype),
            pltpu.SemaphoreType.DMA,
            pltpu.SemaphoreType.DMA((n,)),
            pltpu.SemaphoreType.DMA((4, n)),
        ],
        compiler_params=pltpu.CompilerParams(collective_id=0, has_side_effects=True),
    )(zone, owners, tile)


def lane_box(v):
    lane = lax.broadcasted_iota(jnp.int32, v.shape, v.ndim - 1)
    total = v
    for d in range(1, REACH + 1):
        right = pltpu.roll(v, d, v.ndim - 1)
        left = pltpu.roll(v, W - d, v.ndim - 1)
        total = total + jnp.where(lane >= d, right, 0.0) + jnp.where(lane < W - d, left, 0.0)
    return total


def rotate_rows(v, bits, sign):
    for k in range(4):
        step = 1 << k
        moved = pltpu.roll(v, (16 - step) if sign < 0 else step, v.ndim - 2)
        v = jnp.where(bits[k], moved, v)
    return v


def conv_taps(tile_f, stack, weights):
    lane = lax.rem(lax.broadcasted_iota(jnp.int32, (C, H * W), 1), W)
    pixels = H * W
    left = jnp.where(lane >= 1, pltpu.roll(tile_f, 1, 1), 0.0).astype(jnp.bfloat16)
    right = jnp.where(lane < W - 1, pltpu.roll(tile_f, pixels - 1, 1), 0.0).astype(jnp.bfloat16)
    views = (left, tile_f.astype(jnp.bfloat16), right)
    zeros = jnp.zeros((C, W), jnp.bfloat16)
    for tap in range(9):
        dy = tap // 3 - 1
        v = views[tap % 3]
        rows = slice(tap * C, (tap + 1) * C)
        if dy == 0:
            stack[rows, :] = v
        elif dy < 0:
            stack[rows, 0:W] = zeros
            stack[rows, W:pixels] = v[:, 0 : pixels - W]
        else:
            stack[rows, 0 : pixels - W] = v[:, W:pixels]
            stack[rows, pixels - W : pixels] = zeros
    return jnp.dot(weights, stack[...], preferred_element_type=jnp.float32)


def inspect_kernel(zone_ref, t_ref, g_ref, mask_ref, k_ref, energy_ref, part_ref, cross, res, stack):
    gt = g_ref[...]
    g_f = gt.astype(jnp.float32).T
    g = g_f.astype(jnp.bfloat16)

    fold_row = lax.broadcasted_iota(jnp.int32, (8, 16, W), 0) * 16 + lax.broadcasted_iota(
        jnp.int32, (8, 16, W), 1
    )
    gap = fold_row - lax.broadcasted_iota(jnp.int32, (8, 16, W), 2)
    near = jnp.logical_and(gap >= -8, gap < 8)
    near_f = jnp.where(near, 1.0, 0.0)
    near_b = near_f.astype(jnp.bfloat16)

    def bits_of(shape):
        spin = lax.broadcasted_iota(jnp.int32, shape, len(shape) - 1) + 8
        return [((spin >> k) & 1) == 1 for k in range(4)]

    bits3 = bits_of((H, 16, W))

    def band(full):
        v = full.reshape(H, 8, 16, W)
        v = jnp.sum(v * near_f[None], axis=1)
        return lane_box(rotate_rows(v, bits3, -1))

    for y in range(H):
        gram = jnp.dot(g, t_ref[:, y * W : (y + 1) * W], preferred_element_type=jnp.float32)
        cross[y] = band(gram)
    square = jnp.sum(g_f * g_f, axis=1, keepdims=True)
    other_rows = band(jnp.broadcast_to(square, (H * W, W)))
    others = [other_rows[r] for r in range(H)]

    t_f = t_ref[...].astype(jnp.float32)
    own = jnp.sum(t_f * t_f, axis=0, keepdims=True)
    own_rows = [own[:, y * W : (y + 1) * W] for y in range(H)]
    row_id = lax.broadcasted_iota(jnp.int32, (16, W), 0)
    used = jnp.logical_and(row_id >= 8 - SHIFT, row_id <= 8 + SHIFT)

    for y in range(H):
        lo_y, hi_y = max(0, y - REACH), min(H - 1, y + REACH)
        self_energy = own_rows[lo_y]
        for r in range(lo_y + 1, hi_y + 1):
            self_energy = self_energy + own_rows[r]
        self_energy = jnp.broadcast_to(lane_box(self_energy), (16, W))
        denom = jnp.zeros((16, W), jnp.float32)
        picked = {}
        for a in range(-SHIFT, SHIFT + 1):
            num = None
            oth = None
            for r in range(lo_y, hi_y + 1):
                if 0 <= r + a < H:
                    num = cross[r, r + a] if num is None else num + cross[r, r + a]
                    oth = others[r + a] if oth is None else oth + others[r + a]
            if num is None:
                expo = jnp.where(used, 1.0, 0.0)
            else:
                logit = (32.0 * num) * lax.rsqrt(self_energy * oth + 1e-05)
                expo = jnp.where(used, jnp.exp(logit), 0.0)
            denom = denom + expo
            if 0 <= y + a < H:
                picked[y + a] = expo
        stacked = jnp.stack(
            [picked[r] if r in picked else jnp.zeros((16, W), jnp.float32) for r in range(H)]
        )
        stacked = rotate_rows(stacked, bits3, 1)
        high = stacked.astype(jnp.bfloat16)
        low = (stacked - high.astype(jnp.float32)).astype(jnp.bfloat16)
        wide_high = (high[:, None] * near_b[None]).reshape(H * W, W)
        wide_low = (low[:, None] * near_b[None]).reshape(H * W, W)
        numer = jnp.dot(gt, wide_high, preferred_element_type=jnp.float32) + jnp.dot(
            gt, wide_low, preferred_element_type=jnp.float32
        )
        total = jnp.sum(denom, axis=0, keepdims=True)
        aligned = numer / total
        cols = slice(y * W, (y + 1) * W)
        res[:, cols] = (t_f[:, cols] - aligned).astype(jnp.bfloat16).astype(jnp.float32)

    residual = res[...]
    hidden = jnp.maximum(conv_taps(residual, stack, k_ref[0]), 0.0)
    hidden = hidden.astype(jnp.bfloat16).astype(jnp.float32)
    refined = residual + conv_taps(hidden, stack, k_ref[1])
    flat = jnp.sum(refined * refined, axis=0, keepdims=True) * (1.0 / C)
    energy = jnp.concatenate([flat[:, y * W : (y + 1) * W] for y in range(H)], axis=0)
    energy_ref[...] = energy
    masked = mask_ref[...].astype(jnp.float32)
    die_sum = jnp.sum(jnp.sum(energy * masked, axis=1, keepdims=True), axis=0, keepdims=True)
    die_count = jnp.sum(jnp.sum(masked, axis=1, keepdims=True), axis=0, keepdims=True)
    row8 = lax.broadcasted_iota(jnp.int32, (H, W), 0)
    lane8 = lax.broadcasted_iota(jnp.int32, (H, W), 1)
    pair = jnp.where(row8 == 0, die_sum, die_count)
    part_ref[...] = jnp.where(lane8 == zone_ref[0], pair, 0.0)


def inspect(zone, tile, golden, mask, kernels_t):
    vmem = pl.BlockSpec(memory_space=pltpu.VMEM)
    plane = jax.ShapeDtypeStruct((H, W), jnp.float32)
    return pl.pallas_call(
        inspect_kernel,
        out_shape=(plane, plane),
        in_specs=[pl.BlockSpec(memory_space=pltpu.SMEM), vmem, vmem, vmem, vmem],
        out_specs=(vmem, vmem),
        scratch_shapes=[
            pltpu.VMEM((H, H, 16, W), jnp.float32),
            pltpu.VMEM((C, H * W), jnp.float32),
            pltpu.VMEM((9 * C, H * W), jnp.bfloat16),
        ],
    )(zone, tile, golden, mask, kernels_t)


def score_kernel(n, zone_ref, energy_ref, part_ref, score_ref, parts, send, recv):
    me = lax.axis_index("col")
    barrier = pltpu.get_barrier_semaphore()
    for k in range(1, n):
        pl.semaphore_signal(
            barrier, inc=1, device_id={"col": lax.rem(me + k, n)}, device_id_type=MESH
        )
    pl.semaphore_wait(barrier, n - 1)

    def copy(k):
        return pltpu.make_async_remote_copy(
            src_ref=part_ref,
            dst_ref=parts.at[k],
            send_sem=send.at[k],
            recv_sem=recv.at[k],
            device_id={"col": lax.rem(me + k, n)},
            device_id_type=MESH,
        )

    for k in range(1, n):
        copy(k).start()
    total = part_ref[...]
    for k in range(1, n):
        copy(k).wait_recv()
    for k in range(1, n):
        total = total + parts[k]
    lane = lax.broadcasted_iota(jnp.int32, (H, W), 1)
    mine = jnp.sum(jnp.where(lane == zone_ref[0], total, 0.0), axis=1, keepdims=True)
    mean = mine[0:1] / jnp.maximum(mine[1:2], 1.0)
    score_ref[...] = energy_ref[...] / (mean + 0.01)
    for k in range(1, n):
        copy(k).wait_send()


def score_of(zone, energy, part, n):
    vmem = pl.BlockSpec(memory_space=pltpu.VMEM)
    return pl.pallas_call(
        functools.partial(score_kernel, n),
        out_shape=jax.ShapeDtypeStruct((H, W), jnp.float32),
        in_specs=[pl.BlockSpec(memory_space=pltpu.SMEM), vmem, vmem],
        out_specs=vmem,
        scratch_shapes=[
            pltpu.VMEM((n, H, W), jnp.float32),
            pltpu.SemaphoreType.DMA((n,)),
            pltpu.SemaphoreType.DMA((n,)),
        ],
        compiler_params=pltpu.CompilerParams(collective_id=1, has_side_effects=True),
    )(zone, energy, part)


def body(n, features, zone_ids, golden_owner, defect_mask, kernels):
    tile = features[0].reshape(H * W, C).T
    kernels_t = jnp.swapaxes(kernels, 1, 2)
    golden = gather_golden(zone_ids, golden_owner, tile, n)
    energy, part = inspect(zone_ids, tile, golden, defect_mask[0], kernels_t)
    return score_of(zone_ids, energy, part, n)[None]


def solution(mesh):
    in_specs = (
        P(("groups", "col"), None, None),
        P(("groups", "col")),
        P("groups"),
        P(("groups", "col"), None, None),
        P(),
    )
    out_specs = P(("groups", "col"), None, None)
    run = functools.partial(body, mesh.shape["col"])
    return jax.shard_map(run, mesh=mesh, in_specs=in_specs, out_specs=out_specs, check_vma=False)
```

time: 425 us -> 41.3 us (0.10)
  local copies, waits for them, and re-layouts: 179 us -> 3.23 us
  other arithmetic: 125 us -> 0 us
  waiting for transfers between devices: 43 us -> 0 us
  Pallas kernels: 0 us -> 37.1 us
  blocking collectives: 31.4 us -> 0 us
  loops' own time: 27.6 us -> 0 us
  between operations: 15 us -> 0.67 us
    reshape x342 -> x0, local copies, waits for them, and re-layouts: 133 us -> none  [the longest x170 73.2 us: channel_sum(): return jnp.sum(values.reshape(values.shape[0], -1, chans), axis=-1)]
    add x197 -> x0, other arithmetic: 51.4 us -> none  [the longest x13 32.5 us: row_step(): numer = numer + jnp.repeat(expo, chans, axis=1) * moved]
    all_gather x1 -> x0, waiting for transfers between devices: 42.3 us -> none  [body(): piece = lax.all_gather(features, 'col', axis=0, tiled=True)]
    reduce_sum x175 -> x0, other arithmetic: 39.7 us -> none  [the longest x171 35.9 us: channel_sum(): return jnp.sum(values.reshape(values.shape[0], -1, chans), axis=-1)]
    pallas_call x0 -> x3, Pallas kernels: none -> 37.1 us  [the longest x1 24.2 us: gather_golden(): pl.pallas_call(functools.partial(gather_kernel, n, nz, ny), out_shape=jax...]
    broadcast_in_dim x170 -> x0, local copies, waits for them, and re-layouts: 32.5 us -> none  [the longest x169 32.3 us: row_step(): numer = numer + jnp.repeat(expo, chans, axis=1) * moved]
    psum x1 -> x0, blocking collectives: 31.4 us -> none  [body(): lax.psum((onehot * die_sum, onehot * die_count), 'col')]
    another operation x1 -> x0, loops' own time: 27.6 us -> none  [align_golden(): lax.scan(row_step, start, jnp.arange(side, dtype=jnp.int32))]
  transfers between devices with their start and end apart: 1 -> 0, of which waited for: 1 -> 0; matrix products, arithmetic and copies ran while one was open for 1% -> 0% of each run, Pallas kernels for 0% -> 0%
where the time goes in v1:
time: 41.3 us; the launch traced here: 41 us
  Pallas kernels  37.1 us (90%)
  local copies, waits for them, and re-layouts  3.23 us (8%)
  between operations  0.67 us (2%)
    pallas_call x1, Pallas kernels, gather_golden(): pl.pallas_call(functools.partial(gather_kernel, n, nz, ny), out_shape=jax...  24.2 us
    pallas_call x1, Pallas kernels, score_of(): pl.pallas_call(functools.partial(score_kernel, n), out_shape=jax.ShapeDty...  8.11 us
    pallas_call x1, Pallas kernels, inspect(): pl.pallas_call(inspect_kernel, out_shape=(plane, plane), in_specs=[pl.Blo...  4.81 us
    another operation x2, local copies, waits for them, and re-layouts, body(): tile = features[0].reshape(H * W, C).T  1.97 us
    unnamed x1, local copies, waits for them, and re-layouts  1.26 us

profile of v1, /device:TPU:0, one launch (start us, length us, event | category | flops | bytes accessed | tf_op | source)
XLA Modules:
  0.0 41.0 jit_solution(6246132045028341091)
XLA Ops:
  0.7 1.2 %reshape_squeeze.3 = bf16[1024,64]{1,0:T(8,128)(2,1)S(1)} reshape(bf16[1,8,8192]{2,1,0:T(8,128)(2,1)} %param.5) | data formatting | bytes 262144 | tf_op jit(solution)/shard_map/reshape;squeeze | solution.py:387
  1.8 0.8 %copy.6 = bf16[1024,64]{0,1:T(8,128)(2,1)} copy(bf16[1024,64]{1,0:T(8,128)(2,1)S(1)} %reshape_squeeze.3) | data formatting | bytes 262144 | tf_op jit(solution)/shard_map/reshape;squeeze | solution.py:387
  2.6 24.2 %shard_map.55.g_ref = bf16[64,1024]{1,0:T(8,128)(2,1)} custom-call(s32[1]{0:T(128)S(6)} %copy.8.zone_ref, s32[8]{0:T(128)} %owner_ref.1, bf16[64,1024]{1,0:T(8,128)(2,1)} %bitcast.4), custom_call_target="tpu_custom_call" | custom-call | tf_op jit(solution)/shard_map/pallas_call | solution.py:169
  26.9 4.8 %shard_map.56 = (f32[8,128]{1,0:T(8,128)}, f32[8,128]{1,0:T(8,128)}) custom-call(s32[1]{0:T(128)S(6)} %copy.8.zone_ref, bf16[64,1024]{1,0:T(8,128)(2,1)} %bitcast.5, bf16[64,1024]{1,0:T(8,128)(2,1)} %shard_map.55.g_ref, s32[8,128]{1,0:T(8,128)} %bitcast.8, bf16[2,64,576]{2,1,0:T(8,128)(2,1)} %bitcast.6), custom_call_target="tpu_custom_call" | custom-call | tf_op jit(solution)/shard_map/pallas_call | solution.py:323
  31.7 8.1 %shard_map.57 = f32[8,128]{1,0:T(8,128)} custom-call(s32[1]{0:T(128)S(6)} %copy.8.zone_ref, f32[8,128]{1,0:T(8,128)} %get-tuple-element.7.energy_ref, f32[8,128]{1,0:T(8,128)} %get-tuple-element.8.part_ref), custom_call_target="tpu_custom_call" | custom-call | tf_op jit(solution)/shard_map/pallas_call | solution.py:372
  39.8 1.3 %copy.9 = f32[1,8,128]{2,1,0:T(8,128)} copy(f32[1,8,128]{2,1,0:T(8,128)} %bitcast.7) | data formatting | bytes 8192

commit v2 on v1

v2 whole, which is shorter than its diff:
```python
import functools

import jax
import jax.numpy as jnp
from jax import lax
from jax.experimental import pallas as pl
from jax.experimental.pallas import tpu as pltpu
from jax.sharding import PartitionSpec as P

C = 64
H = 8
W = 128
SHIFT = 6
REACH = 2
Z = 8
PARTS = 2
MESH = pl.DeviceIdType.MESH


def lane_box(v):
    lane = lax.broadcasted_iota(jnp.int32, v.shape, v.ndim - 1)
    total = v
    for d in range(1, REACH + 1):
        right = pltpu.roll(v, d, v.ndim - 1)
        left = pltpu.roll(v, W - d, v.ndim - 1)
        total = total + jnp.where(lane >= d, right, 0.0) + jnp.where(lane < W - d, left, 0.0)
    return total


def rotate_rows(v, bits, sign):
    for k in range(4):
        step = 1 << k
        moved = pltpu.roll(v, (16 - step) if sign < 0 else step, v.ndim - 2)
        v = jnp.where(bits[k], moved, v)
    return v


def conv_taps(tile_f, stack, weights):
    lane = lax.rem(lax.broadcasted_iota(jnp.int32, (C, H * W), 1), W)
    pixels = H * W
    left = jnp.where(lane >= 1, pltpu.roll(tile_f, 1, 1), 0.0).astype(jnp.bfloat16)
    right = jnp.where(lane < W - 1, pltpu.roll(tile_f, pixels - 1, 1), 0.0).astype(jnp.bfloat16)
    views = (left, tile_f.astype(jnp.bfloat16), right)
    zeros = jnp.zeros((C, W), jnp.bfloat16)
    for tap in range(9):
        dy = tap // 3 - 1
        v = views[tap % 3]
        rows = slice(tap * C, (tap + 1) * C)
        if dy == 0:
            stack[rows, :] = v
        elif dy < 0:
            stack[rows, 0:W] = zeros
            stack[rows, W:pixels] = v[:, 0 : pixels - W]
        else:
            stack[rows, 0 : pixels - W] = v[:, W:pixels]
            stack[rows, pixels - W : pixels] = zeros
    return jnp.dot(weights, stack[...], preferred_element_type=jnp.float32)


def to_pixels(pieces, rows, pixels):
    wide = pieces[0].shape[1] // 128
    for k in range(PARTS):
        for j in range(wide):
            at = (k * wide + j) * H
            rows[at : at + H, :] = pieces[k][:, j * 128 : (j + 1) * 128].astype(jnp.float32)
    pairs = W * C // 128
    for y in range(H):
        v = rows[pl.ds(y, pairs, stride=H), :]
        pixels[pl.ds(y * W, pairs, stride=2), :] = v
        pixels[pl.ds(y * W + 1, pairs, stride=2), :] = pltpu.roll(v, C, 1)
    return pixels[:, 0:C]


def whole_kernel(
    n, nz, ny,
    zone_ref, owner_ref, feat_ref, mask_ref, k_ref, score_ref,
    slots, rows, pixels, t_ref, kt_ref, cross, res, stack, part, parts,
    own_sem, recv, sends, part_send, part_recv,
):
    me = lax.axis_index("col")
    core = lax.rem(me, 2)
    yy = lax.rem(me // 2, ny)
    zz = me // (2 * ny)

    def idx(z, y, c):
        return (z * ny + y) * 2 + c

    up = idx(zz + 1, yy, core)
    down = idx(zz - 1, yy, core)
    side = idx(zz, 1 - yy, core)
    mate = idx(zz, yy, 1 - core)
    has_up = zz + 1 < nz
    has_down = zz > 0

    barrier = pltpu.get_barrier_semaphore()

    def greet(dev):
        pl.semaphore_signal(barrier, inc=1, device_id={"col": dev}, device_id_type=MESH)

    @pl.when(has_up)
    def _():
        greet(up)

    @pl.when(has_down)
    def _():
        greet(down)

    if ny == 2:
        greet(side)
    greet(mate)
    peers = ny + jnp.where(has_up, 1, 0) + jnp.where(has_down, 1, 0)
    pl.semaphore_wait(barrier, peers)

    span = feat_ref.shape[2] // PARTS

    def copy(kind, slot, k, dev, own=False):
        return pltpu.make_async_remote_copy(
            src_ref=feat_ref.at[0, :, pl.ds(k * span, span)] if own else slots.at[slot, k],
            dst_ref=slots.at[slot, k],
            send_sem=sends.at[kind, slot, k],
            recv_sem=recv.at[slot, k],
            device_id={"col": dev},
            device_id_type=MESH,
        )

    def arrive(slot, k):
        copy(0, slot, k, mate).wait_recv()

    def own_copy(k):
        return pltpu.make_async_copy(
            feat_ref.at[0, :, pl.ds(k * span, span)], slots.at[me, k], own_sem.at[k]
        )

    for k in range(PARTS):

        @pl.when(has_up)
        def _():
            copy(0, me, k, up, True).start()

        @pl.when(has_down)
        def _():
            copy(1, me, k, down, True).start()

        if ny == 2:
            copy(2, me, k, side, True).start()
        copy(3, me, k, mate, True).start()
        own_copy(k).start()

    test = to_pixels([feat_ref[0, :, k * span : (k + 1) * span] for k in range(PARTS)], rows, pixels)
    t_f = test.T
    t_ref[...] = t_f
    for i in range(2):
        kt_ref[i] = k_ref[i].astype(jnp.float32).T.astype(jnp.bfloat16)

    def from_side(z, k):
        slot = idx(z, 1 - yy, core)
        arrive(slot, k)
        copy(3, slot, k, mate).start()

    for s in range(1, nz + 1):
        for k in range(PARTS):
            if s < nz:

                @pl.when(zz - s >= 0)
                def _():
                    slot = idx(zz - s, yy, core)
                    arrive(slot, k)

                    @pl.when(has_up)
                    def _():
                        copy(0, slot, k, up).start()

                    if ny == 2:
                        copy(2, slot, k, side).start()
                    copy(3, slot, k, mate).start()

                @pl.when(zz + s < nz)
                def _():
                    slot = idx(zz + s, yy, core)
                    arrive(slot, k)

                    @pl.when(has_down)
                    def _():
                        copy(1, slot, k, down).start()

                    if ny == 2:
                        copy(2, slot, k, side).start()
                    copy(3, slot, k, mate).start()

            if ny == 2:
                if s == 1:
                    from_side(zz, k)
                else:

                    @pl.when(zz - (s - 1) >= 0)
                    def _():
                        from_side(zz - (s - 1), k)

                    @pl.when(zz + (s - 1) < nz)
                    def _():
                        from_side(zz + (s - 1), k)

    for z in range(nz):
        for y in range(ny):
            for k in range(PARTS):
                arrive(idx(z, y, 1 - core), k)
    for k in range(PARTS):
        own_copy(k).wait()

    chosen = slots[owner_ref[zone_ref[0]]]
    g_f = to_pixels([chosen[k] for k in range(PARTS)], rows, pixels)
    g = g_f.astype(jnp.bfloat16)
    gt = g_f.T.astype(jnp.bfloat16)
    fold_row = lax.broadcasted_iota(jnp.int32, (8, 16, W), 0) * 16 + lax.broadcasted_iota(
        jnp.int32, (8, 16, W), 1
    )
    gap = fold_row - lax.broadcasted_iota(jnp.int32, (8, 16, W), 2)
    near = jnp.logical_and(gap >= -8, gap < 8)
    near_f = jnp.where(near, 1.0, 0.0)
    near_b = near_f.astype(jnp.bfloat16)

    def bits_of(shape):
        spin = lax.broadcasted_iota(jnp.int32, shape, len(shape) - 1) + 8
        return [((spin >> k) & 1) == 1 for k in range(4)]

    bits3 = bits_of((H, 16, W))

    def band(full):
        v = full.reshape(H, 8, 16, W)
        v = jnp.sum(v * near_f[None], axis=1)
        return lane_box(rotate_rows(v, bits3, -1))

    for y in range(H):
        gram = jnp.dot(g, t_ref[:, y * W : (y + 1) * W].astype(jnp.bfloat16), preferred_element_type=jnp.float32)
        cross[y] = band(gram)
    square = jnp.sum(g_f * g_f, axis=1, keepdims=True)
    other_rows = band(jnp.broadcast_to(square, (H * W, W)))
    others = [other_rows[r] for r in range(H)]

    t_f = t_ref[...]
    own = jnp.sum(t_f * t_f, axis=0, keepdims=True)
    own_rows = [own[:, y * W : (y + 1) * W] for y in range(H)]
    row_id = lax.broadcasted_iota(jnp.int32, (16, W), 0)
    used = jnp.logical_and(row_id >= 8 - SHIFT, row_id <= 8 + SHIFT)

    for y in range(H):
        lo_y, hi_y = max(0, y - REACH), min(H - 1, y + REACH)
        self_energy = own_rows[lo_y]
        for r in range(lo_y + 1, hi_y + 1):
            self_energy = self_energy + own_rows[r]
        self_energy = jnp.broadcast_to(lane_box(self_energy), (16, W))
        denom = jnp.zeros((16, W), jnp.float32)
        picked = {}
        for a in range(-SHIFT, SHIFT + 1):
            num = None
            oth = None
            for r in range(lo_y, hi_y + 1):
                if 0 <= r + a < H:
                    num = cross[r, r + a] if num is None else num + cross[r, r + a]
                    oth = others[r + a] if oth is None else oth + others[r + a]
            if num is None:
                expo = jnp.where(used, 1.0, 0.0)
            else:
                logit = (32.0 * num) * lax.rsqrt(self_energy * oth + 1e-05)
                expo = jnp.where(used, jnp.exp(logit), 0.0)
            denom = denom + expo
            if 0 <= y + a < H:
                picked[y + a] = expo
        stacked = jnp.stack(
            [picked[r] if r in picked else jnp.zeros((16, W), jnp.float32) for r in range(H)]
        )
        stacked = rotate_rows(stacked, bits3, 1)
        high = stacked.astype(jnp.bfloat16)
        low = (stacked - high.astype(jnp.float32)).astype(jnp.bfloat16)
        wide_high = (high[:, None] * near_b[None]).reshape(H * W, W)
        wide_low = (low[:, None] * near_b[None]).reshape(H * W, W)
        numer = jnp.dot(gt, wide_high, preferred_element_type=jnp.float32) + jnp.dot(
            gt, wide_low, preferred_element_type=jnp.float32
        )
        total = jnp.sum(denom, axis=0, keepdims=True)
        aligned = numer / total
        cols = slice(y * W, (y + 1) * W)
        res[:, cols] = (t_f[:, cols] - aligned).astype(jnp.bfloat16).astype(jnp.float32)

    residual = res[...]
    hidden = jnp.maximum(conv_taps(residual, stack, kt_ref[0]), 0.0)
    hidden = hidden.astype(jnp.bfloat16).astype(jnp.float32)
    refined = residual + conv_taps(hidden, stack, kt_ref[1])
    flat = jnp.sum(refined * refined, axis=0, keepdims=True) * (1.0 / C)
    energy = jnp.concatenate([flat[:, y * W : (y + 1) * W] for y in range(H)], axis=0)
    masked = mask_ref[0].astype(jnp.float32)
    die_sum = jnp.sum(jnp.sum(energy * masked, axis=1, keepdims=True), axis=0, keepdims=True)
    die_count = jnp.sum(jnp.sum(masked, axis=1, keepdims=True), axis=0, keepdims=True)
    lane = lax.broadcasted_iota(jnp.int32, (1, W), 1)
    zone = zone_ref[0]
    at_sum = lane == zone
    at_count = lane == zone + W // 2
    mine = jnp.where(at_sum, die_sum, jnp.where(at_count, die_count, 0.0))
    part[...] = mine

    def give(k):
        return pltpu.make_async_remote_copy(
            src_ref=part,
            dst_ref=parts.at[k],
            send_sem=part_send.at[k],
            recv_sem=part_recv.at[k],
            device_id={"col": lax.rem(me + k, n)},
            device_id_type=MESH,
        )

    for k in range(1, n):
        give(k).start()

    def sent(kind, slot, k):
        copy(kind, slot, k, mate).wait_send()

    for z in range(nz):
        slot = idx(z, yy, core)
        for k in range(PARTS):

            @pl.when(jnp.logical_and(has_up, z <= zz))
            def _():
                sent(0, slot, k)

            @pl.when(jnp.logical_and(has_down, z >= zz))
            def _():
                sent(1, slot, k)

            if ny == 2:
                sent(2, slot, k)
            for y in range(ny):
                sent(3, idx(z, y, core), k)

    for k in range(1, n):
        give(k).wait_recv()
    total = mine
    for k in range(1, n):
        total = total + parts[k]
    zone_sum = jnp.sum(jnp.where(at_sum, total, 0.0), axis=1, keepdims=True)
    zone_count = jnp.sum(jnp.where(at_count, total, 0.0), axis=1, keepdims=True)
    mean = zone_sum / jnp.maximum(zone_count, 1.0)
    score_ref[0] = energy / (mean + 0.01)
    for k in range(1, n):
        give(k).wait_send()


def body(n, features, zone_ids, golden_owner, defect_mask, kernels):
    ny = 2 if n == 16 else 1
    nz = n // (2 * ny)
    vmem = pl.BlockSpec(memory_space=pltpu.VMEM)
    smem = pl.BlockSpec(memory_space=pltpu.SMEM)
    dma = pltpu.SemaphoreType.DMA
    span = W * C // PARTS
    return pl.pallas_call(
        functools.partial(whole_kernel, n, nz, ny),
        out_shape=jax.ShapeDtypeStruct((1, H, W), jnp.float32),
        in_specs=[smem, smem, vmem, vmem, vmem],
        out_specs=vmem,
        scratch_shapes=[
            pltpu.VMEM((n, PARTS, H, span), jnp.bfloat16),
            pltpu.VMEM((H * W * C // 128, 128), jnp.float32),
            pltpu.VMEM((H * W, 128), jnp.float32),
            pltpu.VMEM((C, H * W), jnp.float32),
            pltpu.VMEM((2, C, 9 * C), jnp.bfloat16),
            pltpu.VMEM((H, H, 16, W), jnp.float32),
            pltpu.VMEM((C, H * W), jnp.float32),
            pltpu.VMEM((9 * C, H * W), jnp.bfloat16),
            pltpu.VMEM((1, W), jnp.float32),
            pltpu.VMEM((n, 1, W), jnp.float32),
            dma((PARTS,)),
            dma((n, PARTS)),
            dma((4, n, PARTS)),
            dma((n,)),
            dma((n,)),
        ],
        compiler_params=pltpu.CompilerParams(collective_id=0, has_side_effects=True),
    )(zone_ids, golden_owner, features, defect_mask, kernels)


def solution(mesh):
    in_specs = (
        P(("groups", "col"), None, None),
        P(("groups", "col")),
        P("groups"),
        P(("groups", "col"), None, None),
        P(),
    )
    out_specs = P(("groups", "col"), None, None)
    run = functools.partial(body, mesh.shape["col"])
    return jax.shard_map(run, mesh=mesh, in_specs=in_specs, out_specs=out_specs, check_vma=False)
```

time: 41.3 us -> 35 us (0.85)
  Pallas kernels: 37.1 us -> 31.1 us
    pallas_call x3 -> x1, Pallas kernels: 37.1 us -> 31.1 us  [body(): pl.pallas_call(functools.partial(whole_kernel, n, nz, ny), out_shape=jax....]
    another operation x2 -> x0, local copies, waits for them, and re-layouts: 1.97 us -> none  [body(): tile = features[0].reshape(H * W, C).T]
    unnamed x1 -> x2, local copies, waits for them, and re-layouts: 1.26 us -> 3.05 us
where the time goes in v2:
time: 35 us; the launch traced here: 34.8 us
  Pallas kernels  31.1 us (89%)
  local copies, waits for them, and re-layouts  3.05 us (9%)
  between operations  0.66 us (2%)
    pallas_call x1, Pallas kernels, body(): pl.pallas_call(functools.partial(whole_kernel, n, nz, ny), out_shape=jax....  31.1 us
    unnamed x2, local copies, waits for them, and re-layouts  3.05 us

profile of v2, /device:TPU:0, one launch (start us, length us, event | category | flops | bytes accessed | tf_op | source)
XLA Modules:
  0.0 34.8 jit_solution(12265683613266441061)
XLA Ops:
  0.7 1.8 %copy.6.k_ref = bf16[2,576,64]{2,1,0:T(8,128)(2,1)} copy(bf16[2,576,64]{1,2,0:T(8,128)(2,1)} %param.9) | data formatting | bytes 294912 | tf_op args[4]
  2.4 31.1 %shard_map.55 = f32[1,8,128]{2,1,0:T(8,128)} custom-call(s32[1]{0:T(128)S(6)} %copy.8.zone_ref, s32[8]{0:T(128)} %owner_ref.1, bf16[1,8,8192]{2,1,0:T(8,128)(2,1)} %feat_ref.1, s32[1,8,128]{2,1,0:T(8,128)} %mask_ref.1, bf16[2,576,64]{2,1,0:T(8,128)(2,1)} %copy.6.k_ref), custom_call_target="tpu_custom_call" | custom-call | tf_op jit(solution)/shard_map/pallas_call | solution.py:354
  33.5 1.3 %copy.9 = f32[1,8,128]{2,1,0:T(8,128)} copy(f32[1,8,128]{2,1,0:T(8,128)} %shard_map.55) | data formatting | bytes 8192

commit v3 on v2

--- a/solution.py
+++ b/solution.py
@@ -74,7 +74,7 @@
 def whole_kernel(
     n, nz, ny,
     zone_ref, owner_ref, feat_ref, mask_ref, k_ref, score_ref,
-    slots, rows, pixels, t_ref, kt_ref, cross, res, stack, part, parts,
+    slots, rows, pixels, t_ref, cross, res, stack, part, parts,
     own_sem, recv, sends, part_send, part_recv,
 ):
     me = lax.axis_index("col")
@@ -149,8 +149,6 @@
     test = to_pixels([feat_ref[0, :, k * span : (k + 1) * span] for k in range(PARTS)], rows, pixels)
     t_f = test.T
     t_ref[...] = t_f
-    for i in range(2):
-        kt_ref[i] = k_ref[i].astype(jnp.float32).T.astype(jnp.bfloat16)
 
     def from_side(z, k):
         slot = idx(z, 1 - yy, core)
@@ -283,9 +281,9 @@
         res[:, cols] = (t_f[:, cols] - aligned).astype(jnp.bfloat16).astype(jnp.float32)
 
     residual = res[...]
-    hidden = jnp.maximum(conv_taps(residual, stack, kt_ref[0]), 0.0)
+    hidden = jnp.maximum(conv_taps(residual, stack, k_ref[0]), 0.0)
     hidden = hidden.astype(jnp.bfloat16).astype(jnp.float32)
-    refined = residual + conv_taps(hidden, stack, kt_ref[1])
+    refined = residual + conv_taps(hidden, stack, k_ref[1])
     flat = jnp.sum(refined * refined, axis=0, keepdims=True) * (1.0 / C)
     energy = jnp.concatenate([flat[:, y * W : (y + 1) * W] for y in range(H)], axis=0)
     masked = mask_ref[0].astype(jnp.float32)
@@ -361,7 +359,6 @@
             pltpu.VMEM((H * W * C // 128, 128), jnp.float32),
             pltpu.VMEM((H * W, 128), jnp.float32),
             pltpu.VMEM((C, H * W), jnp.float32),
-            pltpu.VMEM((2, C, 9 * C), jnp.bfloat16),
             pltpu.VMEM((H, H, 16, W), jnp.float32),
             pltpu.VMEM((C, H * W), jnp.float32),
             pltpu.VMEM((9 * C, H * W), jnp.bfloat16),
@@ -374,7 +371,7 @@
             dma((n,)),
         ],
         compiler_params=pltpu.CompilerParams(collective_id=0, has_side_effects=True),
-    )(zone_ids, golden_owner, features, defect_mask, kernels)
+    )(zone_ids, golden_owner, features, defect_mask, jnp.swapaxes(kernels, 1, 2))
 
 
 def solution(mesh):

time: 35 us -> 33.1 us (0.946)
  local copies, waits for them, and re-layouts: 3.05 us -> 1.28 us
    unnamed x2 -> x1, local copies, waits for them, and re-layouts: 3.05 us -> 1.28 us
where the time goes in v3:
time: 33.1 us; the launch traced here: 33 us
  Pallas kernels  31 us (94%)
  local copies, waits for them, and re-layouts  1.28 us (4%)
  between operations  0.66 us (2%)
    pallas_call x1, Pallas kernels, body(): pl.pallas_call(functools.partial(whole_kernel, n, nz, ny), out_shape=jax....  31 us
    unnamed x1, local copies, waits for them, and re-layouts  1.28 us

profile of v3, /device:TPU:0, one launch (start us, length us, event | category | flops | bytes accessed | tf_op | source)
XLA Modules:
  0.0 33.0 jit_solution(5462971277529823859)
XLA Ops:
  0.7 31.0 %shard_map.55 = f32[1,8,128]{2,1,0:T(8,128)} custom-call(s32[1]{0:T(128)S(6)} %copy.7.zone_ref, s32[8]{0:T(128)} %owner_ref.1, bf16[1,8,8192]{2,1,0:T(8,128)(2,1)} %feat_ref.1, s32[1,8,128]{2,1,0:T(8,128)} %mask_ref.1, bf16[2,64,576]{2,1,0:T(8,128)(2,1)} %bitcast.1), custom_call_target="tpu_custom_call" | custom-call | tf_op jit(solution)/shard_map/pallas_call | solution.py:352
  31.7 1.3 %copy.8 = f32[1,8,128]{2,1,0:T(8,128)} copy(f32[1,8,128]{2,1,0:T(8,128)} %shard_map.55) | data formatting | bytes 8192

commit v4 on v3

--- a/solution.py
+++ b/solution.py
@@ -13,7 +13,7 @@
 SHIFT = 6
 REACH = 2
 Z = 8
-PARTS = 2
+PARTS = 1
 MESH = pl.DeviceIdType.MESH
 
 

time: 33.1 us -> 32 us (0.967)
  Pallas kernels: 31 us -> 29.9 us
    pallas_call x1, Pallas kernels: 31 us -> 29.9 us  [body(): pl.pallas_call(functools.partial(whole_kernel, n, nz, ny), out_shape=jax....]
where the time goes in v4:
time: 32 us; the launch traced here: 31.8 us
  Pallas kernels  29.9 us (93%)
  local copies, waits for them, and re-layouts  1.28 us (4%)
  between operations  0.66 us (2%)
    pallas_call x1, Pallas kernels, body(): pl.pallas_call(functools.partial(whole_kernel, n, nz, ny), out_shape=jax....  29.9 us
    unnamed x1, local copies, waits for them, and re-layouts  1.28 us

profile of v4, /device:TPU:0, one launch (start us, length us, event | category | flops | bytes accessed | tf_op | source)
XLA Modules:
  0.0 31.8 jit_solution(5568059845327058317)
XLA Ops:
  0.7 29.9 %shard_map.55 = f32[1,8,128]{2,1,0:T(8,128)} custom-call(s32[1]{0:T(128)S(6)} %copy.7.zone_ref, s32[8]{0:T(128)} %owner_ref.1, bf16[1,8,8192]{2,1,0:T(8,128)(2,1)} %feat_ref.1, s32[1,8,128]{2,1,0:T(8,128)} %mask_ref.1, bf16[2,64,576]{2,1,0:T(8,128)(2,1)} %bitcast.1), custom_call_target="tpu_custom_call" | custom-call | tf_op jit(solution)/shard_map/pallas_call | solution.py:352
  30.6 1.3 %copy.8 = f32[1,8,128]{2,1,0:T(8,128)} copy(f32[1,8,128]{2,1,0:T(8,128)} %shard_map.55) | data formatting | bytes 8192
